TPU v7x, 32 devices: a whole 2x2x4 slice. The times are simulated.
32 devices in a mesh: pp: 4 (over y, core), cp: 4 (over z), tp: 2 (over x).
Axes of the slice: x: 2, y: 2, z: 4, core: 2. Of those that a mesh axis runs over, the one named last changes fastest.
Arguments:
- queries: bfloat16 [4, 1024, 8192], P('pp', 'cp', 'tp'), may hold values from -150 to 150
- keys: bfloat16 [4, 1024, 1024], P('pp', 'cp', 'tp'), may hold values from -6 to 6
- values: bfloat16 [4, 1024, 1024], P('pp', 'cp', 'tp'), may hold values from -6 to 6
- span_order: int32 [8], replicated, may hold values from 0 to 7, each once
Outputs:
- forwarded: bfloat16 [4, 1024, 8192], P('pp', ('cp', 'tp'))
All inputs are finite; a program needn't handle non-finite values.
Results may differ from a plain program's by a relative error of at most 0.005.
Values may be sent and summed in bfloat16 or wider, within the bound.
A program may use at most 64 MiB of HBM per device.

v0:
```python
import math
import jax
import jax.numpy as jnp
from jax import lax
from jax.sharding import PartitionSpec as P

HD = 128
SPAN = 128


def passed_along(value, axis, steps):
    count = lax.axis_size(axis)
    pairs = [(source, (source + steps) % count) for source in range(count)]
    return lax.ppermute(value, axis, pairs)


def row_positions(span_order, start, count, span):
    rows = start + jnp.arange(count, dtype=jnp.int32)
    which = rows // span
    table = jnp.arange(span_order.shape[0], dtype=jnp.int32)
    picked = jnp.sum(jnp.where(which[:, None] == table[None, :], span_order[None, :], 0), axis=1)
    return picked * span + rows % span


def attend_block(carry, grouped, key_rows, value_rows, query_pos, key_pos):
    running, total, summed = carry
    score = jnp.einsum("qngd,knd->ngqk", grouped, key_rows, preferred_element_type=jnp.float32)
    score = score * (1.0 / HD**0.5)
    visible = (key_pos[None, :] <= query_pos[:, None])[None, None]
    score = jnp.where(visible, score, jnp.float32(-1e30))
    renewed = jnp.maximum(running, jnp.max(score, axis=-1))
    weight = jnp.where(visible, jnp.exp(score - renewed[..., None]), jnp.float32(0.0))
    fade = jnp.exp(running - renewed)
    total = total * fade + jnp.sum(weight, axis=-1)
    mixed = jnp.einsum(
        "ngqk,knd->ngqd",
        weight.astype(jnp.bfloat16),
        value_rows,
        preferred_element_type=jnp.float32,
    )
    summed = summed * fade[..., None] + mixed
    return (renewed, total, summed)


def attend_rows(carry, grouped, key_part, value_part, start, query_pos, span_order, span):
    count_rows = key_part.shape[0]
    kv_heads = grouped.shape[1]
    step_rows = math.gcd(count_rows, span)

    def one_block(index, state):
        first = index * step_rows
        key_rows = lax.dynamic_slice_in_dim(key_part, first, step_rows, 0).reshape(
            step_rows, kv_heads, HD
        )
        value_rows = lax.dynamic_slice_in_dim(value_part, first, step_rows, 0).reshape(
            step_rows, kv_heads, HD
        )
        key_pos = row_positions(span_order, start + first, step_rows, span)
        return attend_block(state, grouped, key_rows, value_rows, query_pos, key_pos)

    return lax.fori_loop(0, count_rows // step_rows, one_block, carry)


def to_tokens(attended):
    return lax.all_to_all(attended, "tp", split_axis=0, concat_axis=1, tiled=True)


def to_next(attended):
    return passed_along(attended, "pp", 1)


def shards(queries, keys, values, span_order):
    query_rows = queries[0]
    key_local = keys[0]
    value_local = values[0]
    local_rows = query_rows.shape[0]
    span = SPAN
    kv_heads = key_local.shape[1] // HD
    group = query_rows.shape[1] // HD // kv_heads
    my_rank = lax.axis_index("cp")
    ranks = lax.axis_size("cp")
    grouped = query_rows.reshape(local_rows, kv_heads, group, HD)
    query_pos = row_positions(span_order, my_rank * local_rows, local_rows, span)
    start_state = (
        jnp.full((kv_heads, group, local_rows), -1e30, jnp.float32),
        jnp.zeros((kv_heads, group, local_rows), jnp.float32),
        jnp.zeros((kv_heads, group, local_rows, HD), jnp.float32),
    )

    def cycle_step(turn, state):
        carry, stacked = state
        source = (my_rank - turn) % ranks
        carry = attend_rows(
            carry, grouped, stacked[0], stacked[1], source * local_rows, query_pos, span_order, span
        )
        stacked = passed_along(stacked, "cp", 1)
        return (carry, stacked)

    stacked = jnp.stack([key_local, value_local])
    carry, stacked = lax.fori_loop(0, ranks - 1, cycle_step, (start_state, stacked))
    source = (my_rank - (ranks - 1)) % ranks
    carry = attend_rows(
        carry, grouped, stacked[0], stacked[1], source * local_rows, query_pos, span_order, span
    )
    running, total, summed = carry
    attended = (summed / total[..., None]).astype(jnp.bfloat16)
    attended = jnp.transpose(attended, (2, 0, 1, 3)).reshape(local_rows, kv_heads * group * HD)
    result = to_next(to_tokens(attended))
    return result[None]


def solution(mesh):
    in_specs = (P("pp", "cp", "tp"), P("pp", "cp", "tp"), P("pp", "cp", "tp"), P())
    out_specs = P("pp", ("cp", "tp"), None)
    return jax.shard_map(shards, mesh=mesh, in_specs=in_specs, out_specs=out_specs, check_vma=False)
```

profile of v0, /device:TPU:0, one launch (start us, length us, event | category | flops | bytes accessed | tf_op | source)
XLA Modules:
  0.0 148.4 jit_solution(13930984067491431697)
XLA Ops:
  0.8 4.1 %copy.41 = bf16[1,256,4096]{1,2,0:T(8,128)(2,1)} copy(bf16[1,256,4096]{2,1,0:T(8,128)(2,1)} %param.10) | data formatting | bytes 4194304 | tf_op args[0]
  4.9 3.0 %copy.42 = bf16[256,4,8,128]{3,0,2,1:T(8,128)(2,1)S(1)} copy(bf16[256,4,8,128]{0,3,2,1:T(8,128)(2,1)} %bitcast.103) | data formatting | bytes 4194304 | tf_op jit(solution)/shard_map/while | solution.py:100
  9.1 2.4 %broadcast_in_dim.216 = f32[4,8,256,128]{3,2,1,0:T(8,128)} broadcast(f32[]{:T(128)} %constant.334.clone.1), dimensions={} | broadcast | bytes 4194308 | tf_op jit(solution)/shard_map/broadcast_in_dim | solution.py:87
  11.5 55.1 %while.79 = (s32[]{:T(128)}, f32[4,8,256]{2,1,0:T(8,128)S(1)}, f32[4,8,256]{2,1,0:T(8,128)S(1)}, f32[4,8,256,128]{3,2,1,0:T(8,128)}, bf16[2,256,512]{1,2,0:T(8,1...) while((s32[]{:T(128)}, f32[4,8,256]{2,1,0:T(8,128)S(1)}, ...), condition=%wide.region_7.8_spmd, body=%wide.region_1.7_spmd.sunk | while | flops 552655488 | bytes 28709564 | solution.py:100
  12.6 3.0 %collective-permute-start = (bf16[2,256,512]{1,2,0:T(8,128)(2,1)S(1)}, bf16[2,256,512]{1,2,0:T(8,128)(2,1)}, u32[]{:S(2)}, u32[]{:S(2)}) collective-permute-start(bf16[2,256,512]{1,2,0:T(8,128)(2,1)S(1)} %copy.82), channel_id=1, source_target_pairs={{0,2},{2,4},{4,6},{6,0},{1,3},{3,5},{5,7},{7,1},{8,10},{10,12},{12... | collective-permute-start | bytes 1572872 | tf_op jit(solution)/shard_map/while/body/eval_jaxpr/ppermute | solution.py:14
  15.7 15.2 %while.81 = (s32[]{:T(128)}, f32[4,8,256]{2,1,0:T(8,128)S(1)}, f32[4,8,256]{2,1,0:T(8,128)S(1)}, f32[4,8,256,128]{3,2,1,0:T(8,128)}, s32[]{:T(128)}, /*index=5*/...) while((s32[]{:T(128)}, f32[4,8,256]{2,1,0:T(8,128)S(1)}, ...), condition=%wide.region_6.6_spmd, body=%wide.region_2.5_spmd.sunk | while | flops 552655488 | bytes 24514796 | solution.py:61
  18.0 5.3 %multiply_add_fusion.11 = f32[4,8,256,128]{3,2,1,0:T(8,128)} fusion(f32[4,8,256,128]{3,2,1,0:T(8,128)} %get-tuple-element.1191, bf16[128,4,128,1]{0,2,3,1:T(8,128)(2,1)S(1)} %bitcast.98, f32[4,128,256,8]{2,1,3,0:T(8,128)S(1)} %get-tuple-element.1170, f32[4,8,256]{2,1,0:T(8,128)S(1)} %get-tuple-element.1173, f32[4,8,256]{2,1,0:T(8,128)S(1)} %max.22, ...), kind=kOutput, calls=%fused_computation.1.clone.1 | convolution fusion | flops 275775488 | bytes 12812288 | tf_op jit(solution)/shard_map/while/body/eval_jaxpr/while/body/eval_jaxpr/ngqk,knd->ngqd/dot_general | solution.py:35
  25.6 5.3 %multiply_add_fusion.11 = f32[4,8,256,128]{3,2,1,0:T(8,128)} fusion(f32[4,8,256,128]{3,2,1,0:T(8,128)} %get-tuple-element.1191, bf16[128,4,128,1]{0,2,3,1:T(8,128)(2,1)S(1)} %bitcast.98, f32[4,128,256,8]{2,1,3,0:T(8,128)S(1)} %get-tuple-element.1170, f32[4,8,256]{2,1,0:T(8,128)S(1)} %get-tuple-element.1173, f32[4,8,256]{2,1,0:T(8,128)S(1)} %max.22, ...), kind=kOutput, calls=%fused_computation.1.clone.1 | convolution fusion | flops 275775488 | bytes 12812288 | tf_op jit(solution)/shard_map/while/body/eval_jaxpr/while/body/eval_jaxpr/ngqk,knd->ngqd/dot_general | solution.py:35
  31.9 1.6 %collective-permute-start = (bf16[2,256,512]{1,2,0:T(8,128)(2,1)S(1)}, bf16[2,256,512]{1,2,0:T(8,128)(2,1)}, u32[]{:S(2)}, u32[]{:S(2)}) collective-permute-start(bf16[2,256,512]{1,2,0:T(8,128)(2,1)S(1)} %copy.82), channel_id=1, source_target_pairs={{0,2},{2,4},{4,6},{6,0},{1,3},{3,5},{5,7},{7,1},{8,10},{10,12},{12... | collective-permute-start | bytes 1572872 | tf_op jit(solution)/shard_map/while/body/eval_jaxpr/ppermute | solution.py:14
  33.6 15.2 %while.81 = (s32[]{:T(128)}, f32[4,8,256]{2,1,0:T(8,128)S(1)}, f32[4,8,256]{2,1,0:T(8,128)S(1)}, f32[4,8,256,128]{3,2,1,0:T(8,128)}, s32[]{:T(128)}, /*index=5*/...) while((s32[]{:T(128)}, f32[4,8,256]{2,1,0:T(8,128)S(1)}, ...), condition=%wide.region_6.6_spmd, body=%wide.region_2.5_spmd.sunk | while | flops 552655488 | bytes 24514796 | solution.py:61
  35.9 5.3 %multiply_add_fusion.11 = f32[4,8,256,128]{3,2,1,0:T(8,128)} fusion(f32[4,8,256,128]{3,2,1,0:T(8,128)} %get-tuple-element.1191, bf16[128,4,128,1]{0,2,3,1:T(8,128)(2,1)S(1)} %bitcast.98, f32[4,128,256,8]{2,1,3,0:T(8,128)S(1)} %get-tuple-element.1170, f32[4,8,256]{2,1,0:T(8,128)S(1)} %get-tuple-element.1173, f32[4,8,256]{2,1,0:T(8,128)S(1)} %max.22, ...), kind=kOutput, calls=%fused_computation.1.clone.1 | convolution fusion | flops 275775488 | bytes 12812288 | tf_op jit(solution)/shard_map/while/body/eval_jaxpr/while/body/eval_jaxpr/ngqk,knd->ngqd/dot_general | solution.py:35
  43.4 5.3 %multiply_add_fusion.11 = f32[4,8,256,128]{3,2,1,0:T(8,128)} fusion(f32[4,8,256,128]{3,2,1,0:T(8,128)} %get-tuple-element.1191, bf16[128,4,128,1]{0,2,3,1:T(8,128)(2,1)S(1)} %bitcast.98, f32[4,128,256,8]{2,1,3,0:T(8,128)S(1)} %get-tuple-element.1170, f32[4,8,256]{2,1,0:T(8,128)S(1)} %get-tuple-element.1173, f32[4,8,256]{2,1,0:T(8,128)S(1)} %max.22, ...), kind=kOutput, calls=%fused_computation.1.clone.1 | convolution fusion | flops 275775488 | bytes 12812288 | tf_op jit(solution)/shard_map/while/body/eval_jaxpr/while/body/eval_jaxpr/ngqk,knd->ngqd/dot_general | solution.py:35
  51.4 15.2 %while.81 = (s32[]{:T(128)}, f32[4,8,256]{2,1,0:T(8,128)S(1)}, f32[4,8,256]{2,1,0:T(8,128)S(1)}, f32[4,8,256,128]{3,2,1,0:T(8,128)}, s32[]{:T(128)}, /*index=5*/...) while((s32[]{:T(128)}, f32[4,8,256]{2,1,0:T(8,128)S(1)}, ...), condition=%wide.region_6.6_spmd, body=%wide.region_2.5_spmd.sunk | while | flops 552655488 | bytes 24514796 | solution.py:61
  53.7 5.3 %multiply_add_fusion.11 = f32[4,8,256,128]{3,2,1,0:T(8,128)} fusion(f32[4,8,256,128]{3,2,1,0:T(8,128)} %get-tuple-element.1191, bf16[128,4,128,1]{0,2,3,1:T(8,128)(2,1)S(1)} %bitcast.98, f32[4,128,256,8]{2,1,3,0:T(8,128)S(1)} %get-tuple-element.1170, f32[4,8,256]{2,1,0:T(8,128)S(1)} %get-tuple-element.1173, f32[4,8,256]{2,1,0:T(8,128)S(1)} %max.22, ...), kind=kOutput, calls=%fused_computation.1.clone.1 | convolution fusion | flops 275775488 | bytes 12812288 | tf_op jit(solution)/shard_map/while/body/eval_jaxpr/while/body/eval_jaxpr/ngqk,knd->ngqd/dot_general | solution.py:35
  61.3 5.3 %multiply_add_fusion.11 = f32[4,8,256,128]{3,2,1,0:T(8,128)} fusion(f32[4,8,256,128]{3,2,1,0:T(8,128)} %get-tuple-element.1191, bf16[128,4,128,1]{0,2,3,1:T(8,128)(2,1)S(1)} %bitcast.98, f32[4,128,256,8]{2,1,3,0:T(8,128)S(1)} %get-tuple-element.1170, f32[4,8,256]{2,1,0:T(8,128)S(1)} %get-tuple-element.1173, f32[4,8,256]{2,1,0:T(8,128)S(1)} %max.22, ...), kind=kOutput, calls=%fused_computation.1.clone.1 | convolution fusion | flops 275775488 | bytes 12812288 | tf_op jit(solution)/shard_map/while/body/eval_jaxpr/while/body/eval_jaxpr/ngqk,knd->ngqd/dot_general | solution.py:35
  67.7 15.2 %while.80 = (s32[]{:T(128)}, f32[4,8,256]{2,1,0:T(8,128)S(1)}, f32[4,8,256]{2,1,0:T(8,128)S(1)}, f32[4,8,256,128]{3,2,1,0:T(8,128)}, s32[]{:T(128)}, /*index=5*/...) while((s32[]{:T(128)}, f32[4,8,256]{2,1,0:T(8,128)S(1)}, ...), condition=%wide.region_12.13_spmd, body=%wide.region_8.12_spmd.sunk | while | flops 552655488 | bytes 24514796 | solution.py:61
  70.0 5.3 %multiply_add_fusion.9 = f32[4,8,256,128]{3,2,1,0:T(8,128)} fusion(f32[4,8,256,128]{3,2,1,0:T(8,128)} %get-tuple-element.1287, bf16[128,4,128,1]{0,2,3,1:T(8,128)(2,1)S(1)} %bitcast.100, f32[4,128,256,8]{2,1,3,0:T(8,128)S(1)} %get-tuple-element.1154, f32[4,8,256]{2,1,0:T(8,128)S(1)} %get-tuple-element.1157, f32[4,8,256]{2,1,0:T(8,128)S(1)} %max.21, ...), kind=kOutput, calls=%fused_computation.31.clone.1 | convolution fusion | flops 275775488 | bytes 12812288 | tf_op jit(solution)/shard_map/while/body/eval_jaxpr/ngqk,knd->ngqd/dot_general | solution.py:35
  77.6 5.3 %multiply_add_fusion.9 = f32[4,8,256,128]{3,2,1,0:T(8,128)} fusion(f32[4,8,256,128]{3,2,1,0:T(8,128)} %get-tuple-element.1287, bf16[128,4,128,1]{0,2,3,1:T(8,128)(2,1)S(1)} %bitcast.100, f32[4,128,256,8]{2,1,3,0:T(8,128)S(1)} %get-tuple-element.1154, f32[4,8,256]{2,1,0:T(8,128)S(1)} %get-tuple-element.1157, f32[4,8,256]{2,1,0:T(8,128)S(1)} %max.21, ...), kind=kOutput, calls=%fused_computation.31.clone.1 | convolution fusion | flops 275775488 | bytes 12812288 | tf_op jit(solution)/shard_map/while/body/eval_jaxpr/ngqk,knd->ngqd/dot_general | solution.py:35
  82.9 2.9 %fusion.26 = bf16[256,4,8,128]{3,0,2,1:T(8,128)(2,1)S(1)} fusion(f32[4,8,256,128]{3,2,1,0:T(8,128)} %get-tuple-element.809, f32[4,8,256]{2,1,0:T(8,128)S(1)} %get-tuple-element.810), kind=kLoop, calls=%fused_computation.59 | loop fusion | flops 2097152 | bytes 6324224 | tf_op jit(solution)/shard_map/transpose | solution.py:107
  87.2 2.3 %all_to_all.14 = bf16[2,128,4096]{2,1,0:T(8,128)(2,1)} reshape(bf16[256,4,8,128]{3,2,1,0:T(8,128)(2,1)S(1)} %copy.44) | data formatting | bytes 4194304 | tf_op jit(solution)/shard_map/all_to_all | solution.py:65
  89.4 28.0 %all_to_all.19 = bf16[2,128,4096]{2,1,0:T(8,128)(2,1)S(1)} all-to-all(bf16[2,128,4096]{2,1,0:T(8,128)(2,1)} %all_to_all.14), channel_id=1, replica_groups=mesh['pp'=4,'cp'=4,'tp'=2] {'tp'}, dimensions={0} | all-to-all | bytes 4194304 | tf_op jit(solution)/shard_map/all_to_all | solution.py:65
  117.5 2.4 %copy.45 = bf16[128,2,4096]{0,2,1:T(8,128)(2,1)} copy(bf16[128,2,4096]{2,0,1:T(8,128)(2,1)S(1)} %bitcast.102) | data formatting | bytes 4194304 | tf_op jit(solution)/shard_map/all_to_all | solution.py:65
  119.9 25.7 %collective-permute-done.1 = bf16[128,8192]{0,1:T(8,128)(2,1)S(1)} collective-permute-done((bf16[128,8192]{0,1:T(8,128)(2,1)}, bf16[128,8192]{0,1:T(8,128)(2,1)S(1)}, u32[]{:S(2)}, u32[]{:S(2)}) %collective-permute-start.1) | collective-permute-done | bytes 2097184 | tf_op jit(solution)/shard_map/ppermute | solution.py:14
  145.6 2.9 %copy.46 = bf16[1,128,8192]{2,1,0:T(8,128)(2,1)} copy(bf16[1,128,8192]{1,2,0:T(8,128)(2,1)S(1)} %bitcast.105) | data formatting | bytes 4194304 | tf_op jit(solution)/shard_map/broadcast_in_dim | solution.py:109
  (107 shorter events, 26.9 us)
Async XLA Ops:
  0.8 7.2 %copy-start = (bf16[1,256,512]{2,1,0:T(8,128)(2,1)S(1)}, bf16[1,256,512]{2,1,0:T(8,128)(2,1)}, u32[]{:S(2)}) copy-start(bf16[1,256,512]{2,1,0:T(8,128)(2,1)} %param.11) | copy-start | bytes 786436
  0.8 7.3 %copy-start.1 = (bf16[1,256,512]{2,1,0:T(8,128)(2,1)S(1)}, bf16[1,256,512]{2,1,0:T(8,128)(2,1)}, u32[]{:S(2)}) copy-start(bf16[1,256,512]{2,1,0:T(8,128)(2,1)} %param.12) | copy-start | bytes 786436
  8.0 3.6 %copy-start.2 = (s32[8]{0:T(128)S(1)}, s32[8]{0:T(128)}, u32[]{:S(2)}) copy-start(s32[8]{0:T(128)} %param.13) | copy-start | bytes 100
  12.6 18.3 %collective-permute-start = (bf16[2,256,512]{1,2,0:T(8,128)(2,1)S(1)}, bf16[2,256,512]{1,2,0:T(8,128)(2,1)}, u32[]{:S(2)}, u32[]{:S(2)}) collective-permute-start(bf16[2,256,512]{1,2,0:T(8,128)(2,1)S(1)} %copy.82), channel_id=1, source_target_pairs={{0,2},{2,4},{4,6},{6,0},{1,3},{3,5},{5,7},{7,1},{8,10},{10,12},{12... | collective-permute-start | bytes 1572872 | tf_op jit(solution)/shard_map/while/body/eval_jaxpr/ppermute | solution.py:14
  31.9 16.8 %collective-permute-start = (bf16[2,256,512]{1,2,0:T(8,128)(2,1)S(1)}, bf16[2,256,512]{1,2,0:T(8,128)(2,1)}, u32[]{:S(2)}, u32[]{:S(2)}) collective-permute-start(bf16[2,256,512]{1,2,0:T(8,128)(2,1)S(1)} %copy.82), channel_id=1, source_target_pairs={{0,2},{2,4},{4,6},{6,0},{1,3},{3,5},{5,7},{7,1},{8,10},{10,12},{12... | collective-permute-start | bytes 1572872 | tf_op jit(solution)/shard_map/while/body/eval_jaxpr/ppermute | solution.py:14
  49.8 16.8 %collective-permute-start = (bf16[2,256,512]{1,2,0:T(8,128)(2,1)S(1)}, bf16[2,256,512]{1,2,0:T(8,128)(2,1)}, u32[]{:S(2)}, u32[]{:S(2)}) collective-permute-start(bf16[2,256,512]{1,2,0:T(8,128)(2,1)S(1)} %copy.82), channel_id=1, source_target_pairs={{0,2},{2,4},{4,6},{6,0},{1,3},{3,5},{5,7},{7,1},{8,10},{10,12},{12... | collective-permute-start | bytes 1572872 | tf_op jit(solution)/shard_map/while/body/eval_jaxpr/ppermute | solution.py:14
  119.9 25.7 %collective-permute-start.1 = (bf16[128,8192]{0,1:T(8,128)(2,1)}, bf16[128,8192]{0,1:T(8,128)(2,1)S(1)}, u32[]{:S(2)}, u32[]{:S(2)}) collective-permute-start(bf16[128,8192]{0,1:T(8,128)(2,1)} %bitcast.104), channel_id=1, source_target_pairs={{0,8},{8,16},{16,24},{24,0},{1,9},{9,17},{17,25},{25,1},{2,10},{10... | collective-permute-start | bytes 6291464 | tf_op jit(solution)/shard_map/ppermute | solution.py:14
where the time goes:
time: 149 us; the launch traced here: 148 us
  matrix products  49.5 us (33%)
  blocking collectives  28 us (19%)
  waiting for transfers between devices  25.7 us (17%)
  local copies, waits for them, and re-layouts  23.4 us (16%)
  other arithmetic  15 us (10%)
  starting transfers between devices  6.18 us (4%)
    dot_general x8, matrix products, attend_block(): jnp.einsum('ngqk,knd->ngqd', weight.astype(jnp.bfloat16), value_rows, pre...  42.5 us
    all_to_all x1, blocking collectives, to_tokens(): lax.all_to_all(attended, 'tp', split_axis=0, concat_axis=1, tiled=True)  28 us
    ppermute x4, waiting for transfers between devices, passed_along(): return lax.ppermute(value, axis, pairs)  25.7 us
    reduce_sum x8, other arithmetic, attend_block(): total = total * fade + jnp.sum(weight, axis=-1)  8.74 us
    dot_general x8, matrix products, attend_block(): jnp.einsum('qngd,knd->ngqk', grouped, key_rows, preferred_element_type=jn...  6.99 us
    ppermute x4, starting transfers between devices, passed_along(): return lax.ppermute(value, axis, pairs)  6.18 us
    all_to_all x2, local copies, waits for them, and re-layouts, to_tokens(): lax.all_to_all(attended, 'tp', split_axis=0, concat_axis=1, tiled=True)  4.73 us
    unnamed x9, local copies, waits for them, and re-layouts  4.41 us
  transfers between devices with their start and end apart: 4, of which 1 were waited for; matrix products, arithmetic and copies ran while one was open for 31% of the time, Pallas kernels for 0%

commit v1 on v0

--- a/solution.py
+++ b/solution.py
@@ -62,7 +62,13 @@
 
 
 def to_tokens(attended):
-    return lax.all_to_all(attended, "tp", split_axis=0, concat_axis=1, tiled=True)
+    fit_stops_all_on_mesh = lambda tile_in, net_axis: jnp.concatenate(
+        lax.all_to_all(
+            jnp.stack(jnp.split(tile_in, lax.axis_size(net_axis), axis=0)), net_axis, 0, 0
+        ),
+        axis=1,
+    )
+    return fit_stops_all_on_mesh(attended, "tp")
 
 
 def to_next(attended):

time: 149 us -> 149 us (level)
    while x8 -> x9, local copies, waits for them, and re-layouts: 0.03 us -> 5.39 us  [the longest x1 5.37 us: attend_rows(): return lax.fori_loop(0, count_rows // step_rows, one_block, carry)]
    all_to_all x2 -> x0, local copies, waits for them, and re-layouts: 4.73 us -> none  [to_tokens(): lax.all_to_all(attended, 'tp', split_axis=0, concat_axis=1, tiled=True)]
    broadcast_in_dim x1 -> x0, local copies, waits for them, and re-layouts: 2.88 us -> none  [shards(): return result[None]]
    reshape x0 -> x1, local copies, waits for them, and re-layouts: none -> 2.88 us  [to_tokens(): jnp.concatenate(lax.all_to_all(jnp.stack(jnp.split(tile_in, lax.axis_size...]
    unnamed x9 -> x10, local copies, waits for them, and re-layouts: 4.41 us -> 5.73 us
where the time goes in v1:
time: 149 us
  matrix products  49.5 us (33%)
  blocking collectives  26.8 us (18%)
  waiting for transfers between devices  25.7 us (17%)
  local copies, waits for them, and re-layouts  24.6 us (17%)
  other arithmetic  15 us (10%)
  starting transfers between devices  6.18 us (4%)
    dot_general x8, matrix products, attend_block(): jnp.einsum('ngqk,knd->ngqd', weight.astype(jnp.bfloat16), value_rows, pre...  42.5 us
    all_to_all x1, blocking collectives, to_tokens(): lax.all_to_all(jnp.stack(jnp.split(tile_in, lax.axis_size(net_axis), axis...  26.8 us
    ppermute x4, waiting for transfers between devices, passed_along(): return lax.ppermute(value, axis, pairs)  25.7 us
    reduce_sum x8, other arithmetic, attend_block(): total = total * fade + jnp.sum(weight, axis=-1)  8.74 us
    dot_general x8, matrix products, attend_block(): jnp.einsum('qngd,knd->ngqk', grouped, key_rows, preferred_element_type=jn...  6.99 us
    ppermute x4, starting transfers between devices, passed_along(): return lax.ppermute(value, axis, pairs)  6.18 us
    unnamed x10, local copies, waits for them, and re-layouts  5.73 us
    while x1, local copies, waits for them, and re-layouts, attend_rows(): return lax.fori_loop(0, count_rows // step_rows, one_block, carry)  5.37 us
  transfers between devices with their start and end apart: 4, of which 1 were waited for; matrix products, arithmetic and copies ran while one was open for 31% of the time, Pallas kernels for 0%

profile of v1, /device:TPU:0, one launch (start us, length us, event | category | flops | bytes accessed | tf_op | source)
XLA Modules:
  0.0 148.5 jit_solution(11376030599148224738)
XLA Ops:
  0.8 4.1 %copy.28 = bf16[1,256,4096]{1,2,0:T(8,128)(2,1)} copy(bf16[1,256,4096]{2,1,0:T(8,128)(2,1)} %param.10) | data formatting | bytes 4194304 | tf_op args[0]
  4.9 3.0 %copy.29 = bf16[256,4,8,128]{3,0,2,1:T(8,128)(2,1)S(1)} copy(bf16[256,4,8,128]{0,3,2,1:T(8,128)(2,1)} %bitcast.104) | data formatting | bytes 4194304 | tf_op jit(solution)/shard_map/while | solution.py:106
  9.1 2.4 %broadcast_in_dim.216 = f32[4,8,256,128]{3,2,1,0:T(8,128)} broadcast(f32[]{:T(128)} %constant.334.clone.1), dimensions={} | broadcast | bytes 4194308 | tf_op jit(solution)/shard_map/broadcast_in_dim | solution.py:93
  11.5 55.1 %while.79 = (s32[]{:T(128)}, f32[4,8,256]{2,1,0:T(8,128)S(1)}, f32[4,8,256]{2,1,0:T(8,128)S(1)}, f32[4,8,256,128]{3,2,1,0:T(8,128)}, bf16[2,256,512]{1,2,0:T(8,1...) while((s32[]{:T(128)}, f32[4,8,256]{2,1,0:T(8,128)S(1)}, ...), condition=%wide.region_7.8_spmd, body=%wide.region_1.7_spmd.sunk | while | flops 552655488 | bytes 28709564 | solution.py:106
  12.6 3.0 %collective-permute-start = (bf16[2,256,512]{1,2,0:T(8,128)(2,1)S(1)}, bf16[2,256,512]{1,2,0:T(8,128)(2,1)}, u32[]{:S(2)}, u32[]{:S(2)}) collective-permute-start(bf16[2,256,512]{1,2,0:T(8,128)(2,1)S(1)} %copy.68), channel_id=1, source_target_pairs={{0,2},{2,4},{4,6},{6,0},{1,3},{3,5},{5,7},{7,1},{8,10},{10,12},{12... | collective-permute-start | bytes 1572872 | tf_op jit(solution)/shard_map/while/body/eval_jaxpr/ppermute | solution.py:14
  15.7 15.2 %while.81 = (s32[]{:T(128)}, f32[4,8,256]{2,1,0:T(8,128)S(1)}, f32[4,8,256]{2,1,0:T(8,128)S(1)}, f32[4,8,256,128]{3,2,1,0:T(8,128)}, s32[]{:T(128)}, /*index=5*/...) while((s32[]{:T(128)}, f32[4,8,256]{2,1,0:T(8,128)S(1)}, ...), condition=%wide.region_6.6_spmd, body=%wide.region_2.5_spmd.sunk | while | flops 552655488 | bytes 24514796 | solution.py:61
  18.0 5.3 %multiply_add_fusion.11 = f32[4,8,256,128]{3,2,1,0:T(8,128)} fusion(f32[4,8,256,128]{3,2,1,0:T(8,128)} %get-tuple-element.1174, bf16[128,4,128,1]{0,2,3,1:T(8,128)(2,1)S(1)} %bitcast.99, f32[4,128,256,8]{2,1,3,0:T(8,128)S(1)} %get-tuple-element.1153, f32[4,8,256]{2,1,0:T(8,128)S(1)} %get-tuple-element.1156, f32[4,8,256]{2,1,0:T(8,128)S(1)} %max.22, ...), kind=kOutput, calls=%fused_computation.1.clone.1 | convolution fusion | flops 275775488 | bytes 12812288 | tf_op jit(solution)/shard_map/while/body/eval_jaxpr/while/body/eval_jaxpr/ngqk,knd->ngqd/dot_general | solution.py:35
  25.6 5.3 %multiply_add_fusion.11 = f32[4,8,256,128]{3,2,1,0:T(8,128)} fusion(f32[4,8,256,128]{3,2,1,0:T(8,128)} %get-tuple-element.1174, bf16[128,4,128,1]{0,2,3,1:T(8,128)(2,1)S(1)} %bitcast.99, f32[4,128,256,8]{2,1,3,0:T(8,128)S(1)} %get-tuple-element.1153, f32[4,8,256]{2,1,0:T(8,128)S(1)} %get-tuple-element.1156, f32[4,8,256]{2,1,0:T(8,128)S(1)} %max.22, ...), kind=kOutput, calls=%fused_computation.1.clone.1 | convolution fusion | flops 275775488 | bytes 12812288 | tf_op jit(solution)/shard_map/while/body/eval_jaxpr/while/body/eval_jaxpr/ngqk,knd->ngqd/dot_general | solution.py:35
  31.9 1.6 %collective-permute-start = (bf16[2,256,512]{1,2,0:T(8,128)(2,1)S(1)}, bf16[2,256,512]{1,2,0:T(8,128)(2,1)}, u32[]{:S(2)}, u32[]{:S(2)}) collective-permute-start(bf16[2,256,512]{1,2,0:T(8,128)(2,1)S(1)} %copy.68), channel_id=1, source_target_pairs={{0,2},{2,4},{4,6},{6,0},{1,3},{3,5},{5,7},{7,1},{8,10},{10,12},{12... | collective-permute-start | bytes 1572872 | tf_op jit(solution)/shard_map/while/body/eval_jaxpr/ppermute | solution.py:14
  33.6 15.2 %while.81 = (s32[]{:T(128)}, f32[4,8,256]{2,1,0:T(8,128)S(1)}, f32[4,8,256]{2,1,0:T(8,128)S(1)}, f32[4,8,256,128]{3,2,1,0:T(8,128)}, s32[]{:T(128)}, /*index=5*/...) while((s32[]{:T(128)}, f32[4,8,256]{2,1,0:T(8,128)S(1)}, ...), condition=%wide.region_6.6_spmd, body=%wide.region_2.5_spmd.sunk | while | flops 552655488 | bytes 24514796 | solution.py:61
  35.9 5.3 %multiply_add_fusion.11 = f32[4,8,256,128]{3,2,1,0:T(8,128)} fusion(f32[4,8,256,128]{3,2,1,0:T(8,128)} %get-tuple-element.1174, bf16[128,4,128,1]{0,2,3,1:T(8,128)(2,1)S(1)} %bitcast.99, f32[4,128,256,8]{2,1,3,0:T(8,128)S(1)} %get-tuple-element.1153, f32[4,8,256]{2,1,0:T(8,128)S(1)} %get-tuple-element.1156, f32[4,8,256]{2,1,0:T(8,128)S(1)} %max.22, ...), kind=kOutput, calls=%fused_computation.1.clone.1 | convolution fusion | flops 275775488 | bytes 12812288 | tf_op jit(solution)/shard_map/while/body/eval_jaxpr/while/body/eval_jaxpr/ngqk,knd->ngqd/dot_general | solution.py:35
  43.4 5.3 %multiply_add_fusion.11 = f32[4,8,256,128]{3,2,1,0:T(8,128)} fusion(f32[4,8,256,128]{3,2,1,0:T(8,128)} %get-tuple-element.1174, bf16[128,4,128,1]{0,2,3,1:T(8,128)(2,1)S(1)} %bitcast.99, f32[4,128,256,8]{2,1,3,0:T(8,128)S(1)} %get-tuple-element.1153, f32[4,8,256]{2,1,0:T(8,128)S(1)} %get-tuple-element.1156, f32[4,8,256]{2,1,0:T(8,128)S(1)} %max.22, ...), kind=kOutput, calls=%fused_computation.1.clone.1 | convolution fusion | flops 275775488 | bytes 12812288 | tf_op jit(solution)/shard_map/while/body/eval_jaxpr/while/body/eval_jaxpr/ngqk,knd->ngqd/dot_general | solution.py:35
  49.8 1.6 %collective-permute-start = (bf16[2,256,512]{1,2,0:T(8,128)(2,1)S(1)}, bf16[2,256,512]{1,2,0:T(8,128)(2,1)}, u32[]{:S(2)}, u32[]{:S(2)}) collective-permute-start(bf16[2,256,512]{1,2,0:T(8,128)(2,1)S(1)} %copy.68), channel_id=1, source_target_pairs={{0,2},{2,4},{4,6},{6,0},{1,3},{3,5},{5,7},{7,1},{8,10},{10,12},{12... | collective-permute-start | bytes 1572872 | tf_op jit(solution)/shard_map/while/body/eval_jaxpr/ppermute | solution.py:14
  51.4 15.2 %while.81 = (s32[]{:T(128)}, f32[4,8,256]{2,1,0:T(8,128)S(1)}, f32[4,8,256]{2,1,0:T(8,128)S(1)}, f32[4,8,256,128]{3,2,1,0:T(8,128)}, s32[]{:T(128)}, /*index=5*/...) while((s32[]{:T(128)}, f32[4,8,256]{2,1,0:T(8,128)S(1)}, ...), condition=%wide.region_6.6_spmd, body=%wide.region_2.5_spmd.sunk | while | flops 552655488 | bytes 24514796 | solution.py:61
  53.7 5.3 %multiply_add_fusion.11 = f32[4,8,256,128]{3,2,1,0:T(8,128)} fusion(f32[4,8,256,128]{3,2,1,0:T(8,128)} %get-tuple-element.1174, bf16[128,4,128,1]{0,2,3,1:T(8,128)(2,1)S(1)} %bitcast.99, f32[4,128,256,8]{2,1,3,0:T(8,128)S(1)} %get-tuple-element.1153, f32[4,8,256]{2,1,0:T(8,128)S(1)} %get-tuple-element.1156, f32[4,8,256]{2,1,0:T(8,128)S(1)} %max.22, ...), kind=kOutput, calls=%fused_computation.1.clone.1 | convolution fusion | flops 275775488 | bytes 12812288 | tf_op jit(solution)/shard_map/while/body/eval_jaxpr/while/body/eval_jaxpr/ngqk,knd->ngqd/dot_general | solution.py:35
  61.3 5.3 %multiply_add_fusion.11 = f32[4,8,256,128]{3,2,1,0:T(8,128)} fusion(f32[4,8,256,128]{3,2,1,0:T(8,128)} %get-tuple-element.1174, bf16[128,4,128,1]{0,2,3,1:T(8,128)(2,1)S(1)} %bitcast.99, f32[4,128,256,8]{2,1,3,0:T(8,128)S(1)} %get-tuple-element.1153, f32[4,8,256]{2,1,0:T(8,128)S(1)} %get-tuple-element.1156, f32[4,8,256]{2,1,0:T(8,128)S(1)} %max.22, ...), kind=kOutput, calls=%fused_computation.1.clone.1 | convolution fusion | flops 275775488 | bytes 12812288 | tf_op jit(solution)/shard_map/while/body/eval_jaxpr/while/body/eval_jaxpr/ngqk,knd->ngqd/dot_general | solution.py:35
  67.7 15.2 %while.80 = (s32[]{:T(128)}, f32[4,8,256]{2,1,0:T(8,128)S(1)}, f32[4,8,256]{2,1,0:T(8,128)S(1)}, f32[4,8,256,128]{3,2,1,0:T(8,128)}, s32[]{:T(128)}, /*index=5*/...) while((s32[]{:T(128)}, f32[4,8,256]{2,1,0:T(8,128)S(1)}, ...), condition=%wide.region_12.13_spmd, body=%wide.region_8.12_spmd.sunk | while | flops 552655488 | bytes 24514796 | solution.py:61
  70.0 5.3 %multiply_add_fusion.9 = f32[4,8,256,128]{3,2,1,0:T(8,128)} fusion(f32[4,8,256,128]{3,2,1,0:T(8,128)} %get-tuple-element.1270, bf16[128,4,128,1]{0,2,3,1:T(8,128)(2,1)S(1)} %bitcast.101, f32[4,128,256,8]{2,1,3,0:T(8,128)S(1)} %get-tuple-element.1137, f32[4,8,256]{2,1,0:T(8,128)S(1)} %get-tuple-element.1140, f32[4,8,256]{2,1,0:T(8,128)S(1)} %max.21, ...), kind=kOutput, calls=%fused_computation.31.clone.1 | convolution fusion | flops 275775488 | bytes 12812288 | tf_op jit(solution)/shard_map/while/body/eval_jaxpr/ngqk,knd->ngqd/dot_general | solution.py:35
  77.6 5.3 %multiply_add_fusion.9 = f32[4,8,256,128]{3,2,1,0:T(8,128)} fusion(f32[4,8,256,128]{3,2,1,0:T(8,128)} %get-tuple-element.1270, bf16[128,4,128,1]{0,2,3,1:T(8,128)(2,1)S(1)} %bitcast.101, f32[4,128,256,8]{2,1,3,0:T(8,128)S(1)} %get-tuple-element.1137, f32[4,8,256]{2,1,0:T(8,128)S(1)} %get-tuple-element.1140, f32[4,8,256]{2,1,0:T(8,128)S(1)} %max.21, ...), kind=kOutput, calls=%fused_computation.31.clone.1 | convolution fusion | flops 275775488 | bytes 12812288 | tf_op jit(solution)/shard_map/while/body/eval_jaxpr/ngqk,knd->ngqd/dot_general | solution.py:35
  82.9 5.4 %copy.31 = f32[4,8,256,128]{2,3,1,0:T(8,128)} copy(f32[4,8,256,128]{3,2,1,0:T(8,128)} %get-tuple-element.809) | data formatting | bytes 8388608 | tf_op jit(solution)/shard_map/while | solution.py:61
  88.3 2.7 %fusion.26 = bf16[256,4,8,128]{0,3,2,1:T(8,128)(2,1)S(1)} fusion(f32[4,8,256,128]{2,3,1,0:T(8,128)} %copy.31, f32[4,8,256]{2,1,0:T(8,128)S(1)} %get-tuple-element.810), kind=kLoop, calls=%fused_computation.60 | loop fusion | flops 2097152 | bytes 6324224 | tf_op jit(solution)/shard_map/transpose | solution.py:113
  91.8 26.8 %all_to_all.5 = bf16[2,128,4096]{1,2,0:T(8,128)(2,1)S(1)} all-to-all(bf16[2,128,4096]{1,2,0:T(8,128)(2,1)S(1)} %pad_maximum_fusion), channel_id=1, replica_groups=mesh['pp'=4,'cp'=4,'tp'=2] {'tp'}, dimensions={0} | all-to-all | bytes 4194304 | tf_op jit(solution)/shard_map/all_to_all | solution.py:66
  118.6 2.9 %copy.32 = bf16[128,8192]{1,0:T(8,128)(2,1)} copy(bf16[128,8192]{0,1:T(8,128)(2,1)S(1)} %bitcast.103) | data formatting | bytes 4194304 | tf_op jit(solution)/shard_map/reshape | solution.py:65
  121.5 25.7 %collective-permute-done.1 = bf16[128,8192]{1,0:T(8,128)(2,1)S(1)} collective-permute-done((bf16[128,8192]{1,0:T(8,128)(2,1)}, bf16[128,8192]{1,0:T(8,128)(2,1)S(1)}, u32[]{:S(2)}, u32[]{:S(2)}) %collective-permute-start.1) | collective-permute-done | bytes 2097184 | tf_op jit(solution)/shard_map/ppermute | solution.py:14
  (108 shorter events, 26.1 us)
Async XLA Ops:
  0.8 7.2 %copy-start = (bf16[1,256,512]{2,1,0:T(8,128)(2,1)S(1)}, bf16[1,256,512]{2,1,0:T(8,128)(2,1)}, u32[]{:S(2)}) copy-start(bf16[1,256,512]{2,1,0:T(8,128)(2,1)} %param.11) | copy-start | bytes 786436
  0.8 7.3 %copy-start.1 = (bf16[1,256,512]{2,1,0:T(8,128)(2,1)S(1)}, bf16[1,256,512]{2,1,0:T(8,128)(2,1)}, u32[]{:S(2)}) copy-start(bf16[1,256,512]{2,1,0:T(8,128)(2,1)} %param.12) | copy-start | bytes 786436
  8.0 3.6 %copy-start.2 = (s32[8]{0:T(128)S(1)}, s32[8]{0:T(128)}, u32[]{:S(2)}) copy-start(s32[8]{0:T(128)} %param.13) | copy-start | bytes 100
  12.6 18.3 %collective-permute-start = (bf16[2,256,512]{1,2,0:T(8,128)(2,1)S(1)}, bf16[2,256,512]{1,2,0:T(8,128)(2,1)}, u32[]{:S(2)}, u32[]{:S(2)}) collective-permute-start(bf16[2,256,512]{1,2,0:T(8,128)(2,1)S(1)} %copy.68), channel_id=1, source_target_pairs={{0,2},{2,4},{4,6},{6,0},{1,3},{3,5},{5,7},{7,1},{8,10},{10,12},{12... | collective-permute-start | bytes 1572872 | tf_op jit(solution)/shard_map/while/body/eval_jaxpr/ppermute | solution.py:14
  31.9 16.8 %collective-permute-start = (bf16[2,256,512]{1,2,0:T(8,128)(2,1)S(1)}, bf16[2,256,512]{1,2,0:T(8,128)(2,1)}, u32[]{:S(2)}, u32[]{:S(2)}) collective-permute-start(bf16[2,256,512]{1,2,0:T(8,128)(2,1)S(1)} %copy.68), channel_id=1, source_target_pairs={{0,2},{2,4},{4,6},{6,0},{1,3},{3,5},{5,7},{7,1},{8,10},{10,12},{12... | collective-permute-start | bytes 1572872 | tf_op jit(solution)/shard_map/while/body/eval_jaxpr/ppermute | solution.py:14
  49.8 16.8 %collective-permute-start = (bf16[2,256,512]{1,2,0:T(8,128)(2,1)S(1)}, bf16[2,256,512]{1,2,0:T(8,128)(2,1)}, u32[]{:S(2)}, u32[]{:S(2)}) collective-permute-start(bf16[2,256,512]{1,2,0:T(8,128)(2,1)S(1)} %copy.68), channel_id=1, source_target_pairs={{0,2},{2,4},{4,6},{6,0},{1,3},{3,5},{5,7},{7,1},{8,10},{10,12},{12... | collective-permute-start | bytes 1572872 | tf_op jit(solution)/shard_map/while/body/eval_jaxpr/ppermute | solution.py:14
  121.5 25.7 %collective-permute-start.1 = (bf16[128,8192]{1,0:T(8,128)(2,1)}, bf16[128,8192]{1,0:T(8,128)(2,1)S(1)}, u32[]{:S(2)}, u32[]{:S(2)}) collective-permute-start(bf16[128,8192]{1,0:T(8,128)(2,1)} %copy.32), channel_id=1, source_target_pairs={{0,8},{8,16},{16,24},{24,0},{1,9},{9,17},{17,25},{25,1},{2,10},{10... | collective-permute-start | bytes 6291464 | tf_op jit(solution)/shard_map/ppermute | solution.py:14
